TPU v7x, 256 devices: a whole 4x4x8 slice. The times are simulated.
256 devices in a mesh: member: 4 (over y), seq: 64 (over z, x, core).
Axes of the slice: x: 4, y: 4, z: 8, core: 2. Of those that a mesh axis runs over, the one named last changes fastest.
Arguments:
- hidden: bfloat16 [4, 24576, 2880], P('member', 'seq'), may hold values from -6 to 6
- segments: int32 [24576], replicated, may hold values from 0 to 127, never falling along the last dimension, each value on 1 to 768 neighbouring positions
- pre_gain: float32 [4, 2880], P('member'), may hold values from 0.5 to 1.5
- w_query: bfloat16 [4, 2880, 2048], P('member', 'seq'), may hold values from -3 to 3
- w_key: bfloat16 [4, 2880, 256], P('member', 'seq'), may hold values from -3 to 3
- w_value: bfloat16 [4, 2880, 256], P('member', 'seq'), may hold values from -0.109375 to 0.109375
- w_output: bfloat16 [4, 2048, 2880], P('member', 'seq'), may hold values from -0.125 to 0.125
- post_gain: float32 [4, 2880], P('member'), may hold values from 0.5 to 1.5
- final_gain: float32 [4, 2880], P('member'), may hold values from 0.5 to 1.5
- w_judge: bfloat16 [4, 2880, 128], P('member'), may hold values from -0.21875 to 0.21875
Outputs:
- residual_out: bfloat16 [4, 24576, 2880], P('member', 'seq')
- logits: float32 [24576, 128], P('seq')
Inputs may be any that keep to these rules, and one draw needn't show every extreme that they name: `segments`: segment numbers never fall from one token to the next; every number is used, each names 1 to 768 consecutive tokens, and one names exactly 768.
All inputs are finite; a program needn't handle non-finite values.
Results may differ from a plain program's by a relative error of at most 0.014.
Values may be sent and summed in bfloat16 or wider, within the bound.
A program may use at most 128 MiB of HBM per device.

v0:
```python
import math
import jax
import jax.numpy as jnp
from jax import lax
from jax.sharding import PartitionSpec as P

QH = 32
KVH = 4
HD = 64
WINDOW = 128
epsilon = 1e-06
softcap = 50.0
rope_base = 10000.0


def from_behind(block, axis, distance):
    devices = range(lax.axis_size(axis))
    route = [(i - distance, i) for i in devices if i - distance in devices]
    return lax.ppermute(block, axis, route)


def rms_norm(inputs, scale_gain):
    values = inputs.astype(jnp.float32)
    return (
        values * lax.rsqrt(jnp.mean(values * values, axis=-1, keepdims=True) + epsilon) * scale_gain
    )


def rotate(inputs, positions):
    head_size = inputs.shape[-1]
    half_dim = head_size // 2
    frequency = jnp.exp(
        jnp.arange(half_dim, dtype=jnp.float32) * (-2.0 * math.log(rope_base) / head_size)
    )
    angles = positions.astype(jnp.float32)[:, None] * frequency[None, :]
    cosine_term = jnp.cos(angles)[:, None, :]
    sine_term = jnp.sin(angles)[:, None, :]
    lower_half = inputs[..., :half_dim]
    upper_half = inputs[..., half_dim:]
    return jnp.concatenate(
        [
            lower_half * cosine_term - upper_half * sine_term,
            upper_half * cosine_term + lower_half * sine_term,
        ],
        axis=-1,
    )


def attend_heads(block_queries, block_keys, block_values, seg_query, seg_key):
    query_count = block_queries.shape[0]
    key_count = block_keys.shape[0]
    head_span = QH // KVH * HD
    distance = (
        jnp.arange(query_count, dtype=jnp.int32)[:, None]
        + (key_count - query_count)
        - jnp.arange(key_count, dtype=jnp.int32)[None, :]
    )
    allowed = (distance >= 0) & (distance < WINDOW) & (seg_query[:, None] == seg_key[None, :])

    def one_head(head_index):
        query_head = lax.dynamic_slice_in_dim(
            block_queries, head_index * head_span, head_span, 1
        ).reshape(query_count, QH // KVH, HD)
        key_head = lax.dynamic_slice_in_dim(block_keys, head_index * HD, HD, 1)
        value_head = lax.dynamic_slice_in_dim(block_values, head_index * HD, HD, 1)
        scores = jnp.einsum("qgd,kd->gqk", query_head, key_head, preferred_element_type=jnp.float32)
        scores = softcap * jnp.tanh(scores / softcap)
        expanded = jnp.where(allowed[None], jnp.exp(scores), 0.0)
        weights = (expanded / jnp.sum(expanded, axis=-1, keepdims=True)).astype(jnp.bfloat16)
        head_out = jnp.einsum(
            "gqk,kd->qgd", weights, value_head, preferred_element_type=jnp.float32
        )
        return head_out.astype(jnp.bfloat16).reshape(query_count, head_span)

    per_head = lax.map(one_head, jnp.arange(KVH, dtype=jnp.int32))
    return per_head.transpose(1, 0, 2).reshape(query_count, KVH * head_span)


def body(
    hidden, segments, pre_gain, w_query, w_key, w_value, w_output, post_gain, final_gain, w_judge
):
    tok_rows = hidden.shape[1]
    dev_index = lax.axis_index("seq")
    row_first = dev_index * tok_rows
    own_rows = hidden[0]
    normed = rms_norm(own_rows, pre_gain[0]).astype(jnp.bfloat16)
    kv_count = normed.shape[0]
    queries = jnp.dot(
        normed,
        lax.all_gather(w_query[0], "seq", axis=0, tiled=True),
        preferred_element_type=jnp.float32,
    )
    key_rows = jnp.dot(
        normed,
        lax.all_gather(w_key[0], "seq", axis=0, tiled=True),
        preferred_element_type=jnp.float32,
    )
    val_rows = jnp.dot(
        normed,
        lax.all_gather(w_value[0], "seq", axis=0, tiled=True),
        preferred_element_type=jnp.float32,
    )
    query_positions = row_first + jnp.arange(tok_rows, dtype=jnp.int32)
    key_positions = row_first - (kv_count - tok_rows) + jnp.arange(kv_count, dtype=jnp.int32)
    queries = (
        (rotate(queries.reshape(tok_rows, QH, HD), query_positions) * (1.0 / math.sqrt(HD)))
        .astype(jnp.bfloat16)
        .reshape(tok_rows, QH * HD)
    )
    key_rows = (
        rotate(key_rows.reshape(kv_count, KVH, HD), key_positions)
        .astype(jnp.bfloat16)
        .reshape(kv_count, KVH * HD)
    )
    val_rows = val_rows.astype(jnp.bfloat16)
    earlier_keys, earlier_values = from_behind(
        (key_rows[tok_rows - WINDOW :], val_rows[tok_rows - WINDOW :]), "seq", 1
    )
    key_rows = jnp.concatenate([earlier_keys, key_rows], axis=0)
    val_rows = jnp.concatenate([earlier_values, val_rows], axis=0)
    seg_own = lax.dynamic_slice_in_dim(segments, row_first, tok_rows, 0)
    seg_prior = lax.dynamic_slice_in_dim(segments, jnp.maximum(row_first - WINDOW, 0), WINDOW, 0)
    seg_prior = jnp.where(dev_index > 0, seg_prior, -1)
    seg_keys = jnp.concatenate([seg_prior, seg_own], axis=0)
    block_rows = min(tok_rows, 512)

    def one_block(block_number):
        return attend_heads(queries, key_rows, val_rows, seg_own, seg_keys)

    attended = lax.map(one_block, jnp.arange(tok_rows // block_rows, dtype=jnp.int32)).reshape(
        tok_rows, QH * HD
    )
    projected = jnp.dot(
        attended,
        lax.all_gather(w_output[0], "seq", axis=0, tiled=True),
        preferred_element_type=jnp.float32,
    )
    updated = (own_rows.astype(jnp.float32) + rms_norm(projected, post_gain[0])).astype(
        jnp.bfloat16
    )
    closing = rms_norm(updated, final_gain[0]).astype(jnp.bfloat16)
    verdict = jnp.dot(closing, w_judge[0], preferred_element_type=jnp.float32)
    summed_verdict = lax.psum(verdict.astype(jnp.bfloat16), "member").astype(jnp.float32)
    return (updated[None], summed_verdict / lax.axis_size("member"))


def solution(mesh):
    return jax.shard_map(
        body,
        mesh=mesh,
        in_specs=(
            P("member", "seq", None),
            P(),
            P("member", None),
            P("member", "seq", None),
            P("member", "seq", None),
            P("member", "seq", None),
            P("member", "seq", None),
            P("member", None),
            P("member", None),
            P("member", None, None),
        ),
        out_specs=(P("member", "seq", None), P("seq", None)),
        check_vma=False,
    )
```

profile of v0, /device:TPU:2, one launch (start us, length us, event | category | flops | bytes accessed | tf_op | source)
XLA Modules:
  0.0 456.8 jit_solution(2094596954263053369)
XLA Ops:
  7.2 1.5 copy.24
  8.8 0.0 all-gather.11.cloned.1.call-start
  8.9 1.4 copy.25
  10.3 0.0 all-gather.13.cloned.1.call-start
  10.3 2.0 copy.27
  12.3 0.0 all-gather.15.cloned.1.call-start
  12.4 0.5 all-gather.15.cloned.1.call-update
  13.0 0.7 reduce
  13.7 0.7 reduce.1
  14.4 0.7 reduce.2
  15.2 0.8 dynamic_slice.19
  16.0 0.8 broadcast_select_fusion
  16.8 2.2 fusion.27
  19.0 0.3 multiply_cosine_fusion
  19.2 71.9 %all-gather.9.cloned.1.call-done = bf16[1,2880,256]{2,0,1:T(2,128)(2,1)} async-done(((bf16[1,45,256]{2,0,1:T(2,128)(2,1)}), bf16[1,2880,256]{2,0,1:T(2,128)(2,1)}) %all-gather.9.cloned.1.call-update) | async-done | bytes 1474576 | tf_op jit(solution)/shard_map/all_gather | solution.py:100
  91.1 3.2 fusion.45
  94.4 0.7 copy-done.3
  95.1 2.1 collective-permute-start
  97.2 72.0 %all-gather.11.cloned.1.call-done = bf16[1,2880,256]{2,0,1:T(2,128)(2,1)} async-done(((bf16[1,45,256]{2,0,1:T(2,128)(2,1)}), bf16[1,2880,256]{2,0,1:T(2,128)(2,1)}) %all-gather.11.cloned.1.call-update) | async-done | bytes 1474576 | tf_op jit(solution)/shard_map/all_gather | solution.py:95
  169.2 7.3 %copy.34 = bf16[1,2880,256]{1,2,0:T(8,128)(2,1)} copy(bf16[1,2880,256]{2,0,1:T(2,128)(2,1)} %all-gather.11.cloned.1.call-done) | data formatting | bytes 2949120 | tf_op jit(solution)/shard_map/dot_general | solution.py:93
  176.6 2.5 fusion.56
  179.1 0.1 multiply_subtract_fusion.1
  179.1 0.6 slice.31
  179.8 2.3 collective-permute-start.1
  182.1 0.9 pad_maximum_fusion
  183.0 0.8 copy.29
  183.8 3.0 collective-permute-done.1
  186.8 1.6 pad_maximum_fusion.1
  188.4 97.3 %all-gather.13.cloned.1.call-done = bf16[1,2880,2048]{2,0,1:T(2,128)(2,1)} async-done(((bf16[1,45,2048]{2,0,1:T(2,128)(2,1)}), bf16[1,2880,2048]{2,0,1:T(2,128)(2,1)}) %all-gather.13.cloned.1.call-update) | async-done | bytes 11796496 | tf_op jit(solution)/shard_map/all_gather | solution.py:90
  285.6 50.8 %copy.35 = bf16[1,2880,2048]{1,2,0:T(8,128)(2,1)} copy(bf16[1,2880,2048]{2,0,1:T(2,128)(2,1)} %all-gather.13.cloned.1.call-done) | data formatting | bytes 23592960 | tf_op jit(solution)/shard_map/dot_general | solution.py:88
  336.4 9.8 %fusion.54 = f32[384,32,64]{0,2,1:T(8,128)S(1)} fusion(bf16[32,64,2880]{2,1,0:T(8,128)(2,1)} %bitcast.102, bf16[1,384,2880]{1,2,0:T(8,128)(2,1)S(1)} %copy-done.1, f32[2880]{0:T(1024)S(1)} %reduce, f32[384]{0:T(512)S(1)} %copy-done.6), kind=kOutput, calls=%fused_computation.58 | convolution fusion | flops 4534272000 | bytes 17167104 | tf_op jit(solution)/shard_map/dot_general | solution.py:88
  346.2 0.4 multiply_subtract_fusion
  346.7 1.5 fusion.33
  348.2 40.1 %while.18 = (s32[]{:T(128)}, bf16[4,384,512]{1,2,0:T(8,128)(2,1)}, s32[4]{0:T(128)S(1)}, bf16[512,256]{0,1:T(8,128)(2,1)}, bf16[512,256]{0,1:T(8,128)(2,1)}, /*i...) while((s32[]{:T(128)}, bf16[4,384,512]{1,2,0:T(8,128)(2,1)}, ...), condition=%wide.region_3.4_spmd.clone, body=%wide.region_1.3_spmd.clone.sunk | while | flops 418182144 | bytes 15693569 | solution.py:75
  348.2 0.6 dynamic_slice.44
  349.5 1.0 constant_dynamic-slice_fusion.2
  351.2 0.3 fusion.70
  351.5 3.0 fusion.71
  354.5 3.0 fusion.72
  357.5 0.8 constant_dynamic-update-slice_fusion.2
  358.3 0.6 dynamic_slice.44
  359.5 1.0 constant_dynamic-slice_fusion.2
  361.2 0.3 fusion.70
  361.5 3.0 fusion.71
  364.5 3.0 fusion.72
  367.5 0.8 constant_dynamic-update-slice_fusion.2
  368.3 0.6 dynamic_slice.44
  369.5 1.0 constant_dynamic-slice_fusion.2
  371.2 0.3 fusion.70
  371.5 3.0 fusion.71
  374.6 3.0 fusion.72
  377.5 0.8 constant_dynamic-update-slice_fusion.2
  378.3 0.6 dynamic_slice.44
  379.6 1.0 constant_dynamic-slice_fusion.2
  381.3 0.3 fusion.70
  381.6 3.0 fusion.71
  384.6 3.0 fusion.72
  387.6 0.8 constant_dynamic-update-slice_fusion.2
  388.4 10.0 %multiply_reduce_fusion = (f32[384]{0:T(512)S(1)}, f32[384,2880]{0,1:T(8,128)S(1)}) fusion(bf16[384,2048]{0,1:T(8,128)(2,1)} %bitcast.11, bf16[1,2048,2880]{2,1,0:T(8,128)(2,1)} %all-gather.15.cloned.1.call-done), kind=kOutput, calls=%fused_computation.41 | convolution fusion | flops 4532059648 | bytes 17794560 | tf_op jit(solution)/shard_map/dot_general | solution.py:133
  398.3 1.5 fusion.24
  399.8 1.3 copy-done.2
  401.2 2.1 fusion.50
  403.3 45.4 %all-reduce.2.cloned.1.call-done = bf16[384,128]{1,0:T(8,128)(2,1)} async-done(((bf16[384,128]{1,0:T(8,128)(2,1)}), bf16[384,128]{1,0:T(8,128)(2,1)}) %all-reduce.2.cloned.1.call-update) | async-done | bytes 98320 | tf_op jit(solution)/shard_map/psum | solution.py:143
  448.7 1.6 convert_multiply_fusion.3
  (31 shorter events, 0.3 us)
Async XLA Ops:
  7.2 394.0 %copy-start = (bf16[1,2880,128]{2,1,0:T(8,128)(2,1)S(1)}, bf16[1,2880,128]{2,1,0:T(8,128)(2,1)}, u32[]{:S(2)}) copy-start(bf16[1,2880,128]{2,1,0:T(8,128)(2,1)} %param.21) | copy-start | bytes 2211844
  7.2 83.9 %copy-start.1 = (bf16[1,384,2880]{1,2,0:T(8,128)(2,1)S(1)}, bf16[1,384,2880]{1,2,0:T(8,128)(2,1)}, u32[]{:S(2)}) copy-start(bf16[1,384,2880]{1,2,0:T(8,128)(2,1)} %param.12) | copy-start | bytes 6635524
  7.2 83.9 %all-gather.9.cloned.1.call-start = ((), (), s32[]{:S(2)}) async-start(), calls=%async_computation.1 | async-start | bytes 2995200 | tf_op jit(solution)/shard_map/all_gather | solution.py:100
  8.8 160.4 %all-gather.11.cloned.1.call-start = ((), (), s32[]{:S(2)}) async-start(), calls=%async_computation.2 | async-start | bytes 2995200 | tf_op jit(solution)/shard_map/all_gather | solution.py:95
  10.3 275.4 %all-gather.13.cloned.1.call-start = ((), (), s32[]{:S(2)}) async-start(), calls=%async_computation.3 | async-start | bytes 23961600 | tf_op jit(solution)/shard_map/all_gather | solution.py:90
  12.3 376.0 %all-gather.15.cloned.1.call-start = ((), (), s32[]{:S(2)}) async-start(), calls=%async_computation.4 | async-start | bytes 12247040 | tf_op jit(solution)/shard_map/all_gather | solution.py:135
  12.9 435.8 %all-reduce.2.cloned.1.call-start = ((), (), s32[]{:S(2)}) async-start(), calls=%async_computation | async-start | bytes 196608 | tf_op jit(solution)/shard_map/psum | solution.py:143
  19.0 157.6 %copy-start.5 = (f32[384]{0:T(512)}, f32[384]{0:T(512)S(1)}, u32[]{:S(2)}) copy-start(f32[384]{0:T(512)S(1)} %add_rsqrt_fusion.2) | copy-start | bytes 4612
  94.4 0.7 copy-start.3
  95.1 87.0 %collective-permute-start = (bf16[128,256]{1,0:T(8,128)(2,1)S(1)}, bf16[128,256]{1,0:T(8,128)(2,1)}, u32[]{:S(2)}, u32[]{:S(2)}) collective-permute-start(bf16[128,256]{1,0:T(8,128)(2,1)S(1)} %slice.28), channel_id=1, source_target_pairs={{0,1},{1,2},{2,3},{3,4},{4,5},{5,6},{6,7},{7,8},{8,9},{9,10},{10,1... | collective-permute-start | bytes 196616 | tf_op jit(solution)/shard_map/ppermute | solution.py:19
  176.5 5.5 %copy-start.4 = (bf16[384,256]{1,0:T(8,128)(2,1)S(1)}, bf16[384,256]{1,0:T(8,128)(2,1)}, u32[]{:S(2)}) copy-start(bf16[384,256]{1,0:T(8,128)(2,1)} %copy-done.3) | copy-start | bytes 589828
  179.8 7.0 %collective-permute-start.1 = (bf16[128,256]{0,1:T(8,128)(2,1)}, bf16[128,256]{0,1:T(8,128)(2,1)}, u32[]{:S(2)}, u32[]{:S(2)}) collective-permute-start(bf16[128,256]{0,1:T(8,128)(2,1)} %bitcast.5), channel_id=1, source_target_pairs={{0,1},{1,2},{2,3},{3,4},{4,5},{5,6},{6,7},{7,8},{8,9},{9,10},{10,1... | collective-permute-start | bytes 196616 | tf_op jit(solution)/shard_map/ppermute | solution.py:19
  188.4 148.1 %copy-start.6 = (f32[384]{0:T(512)S(1)}, f32[384]{0:T(512)}, u32[]{:S(2)}) copy-start(f32[384]{0:T(512)} %copy-done.5) | copy-start | bytes 4612
  399.8 1.4 copy-start.2
Sparse Core Ops, SparseCore 0:
  11.3 79.8 all-gather.8
  93.8 75.3 all-gather.10
  172.0 113.6 all-gather.12
  288.2 85.5 all-gather.14
  403.4 45.2 all-reduce.1
where the time goes:
time: 460 us; the launch traced here: 457 us
  waiting for transfers between devices  290 us (63%)
  local copies, waits for them, and re-layouts  77 us (17%)
  matrix products  51.6 us (11%)
  other arithmetic  14.2 us (3%)
  between operations  14 us (3%)
  loops' own time  5.31 us (1%)
  starting transfers between devices  4.61 us (1%)
    all_gather x1, waiting for transfers between devices, body(): lax.all_gather(w_query[0], 'seq', axis=0, tiled=True)  97.3 us
    all_gather x1, waiting for transfers between devices, body(): lax.all_gather(w_key[0], 'seq', axis=0, tiled=True)  72 us
    all_gather x1, waiting for transfers between devices, body(): lax.all_gather(w_value[0], 'seq', axis=0, tiled=True)  71.9 us
    dot_general x1, local copies, waits for them, and re-layouts, body(): jnp.dot(normed, lax.all_gather(w_query[0], 'seq', axis=0, tiled=True), pr...  50.8 us
    psum x1, waiting for transfers between devices, body(): lax.psum(verdict.astype(jnp.bfloat16), 'member').astype(jnp.float32)  45.4 us
    dot_general x4, matrix products, one_head(): jnp.einsum('qgd,kd->gqk', query_head, key_head, preferred_element_type=jn...  12.1 us
    dot_general x4, matrix products, one_head(): jnp.einsum('gqk,kd->qgd', weights, value_head, preferred_element_type=jnp...  11.9 us
    dot_general x1, matrix products, body(): jnp.dot(attended, lax.all_gather(w_output[0], 'seq', axis=0, tiled=True),...  9.97 us
  transfers between devices with their start and end apart: 7, of which 5 were waited for; matrix products, arithmetic and copies ran while one was open for 27% of the time, Pallas kernels for 0%

commit v1 on v0

--- a/solution.py
+++ b/solution.py
@@ -87,7 +87,9 @@
     kv_count = normed.shape[0]
     queries = jnp.dot(
         normed,
-        lax.all_gather(w_query[0], "seq", axis=0, tiled=True),
+        jnp.concatenate(
+            lax.all_to_all(jnp.stack([w_query[0]] * lax.axis_size("seq"), 0), "seq", 0, 0), 0
+        ),
         preferred_element_type=jnp.float32,
     )
     key_rows = jnp.dot(

time: 460 us -> 480 us (1.043)
  waiting for transfers between devices: 290 us -> 322 us
  local copies, waits for them, and re-layouts: 77 us -> 58.4 us
  starting transfers between devices: 4.61 us -> 16.7 us
    all_gather x1 -> x0, waiting for transfers between devices: 97.3 us -> none  [body(): lax.all_gather(w_query[0], 'seq', axis=0, tiled=True)]
    all_to_all x0 -> x1, waiting for transfers between devices: none -> 52.2 us  [body(): lax.all_to_all(jnp.stack([w_query[0]] * lax.axis_size('seq'), 0), 'seq',...]
    all_gather x1, waiting for transfers between devices: 71.9 us -> 120 us  [body(): lax.all_gather(w_value[0], 'seq', axis=0, tiled=True)]
    dot_general x1, local copies, waits for them, and re-layouts: 50.8 us -> 16.4 us  [body(): jnp.dot(normed, jnp.concatenate(lax.all_to_all(jnp.stack([w_query[0]] * l...]
    all_gather x1, waiting for transfers between devices: 72 us -> 98.9 us  [body(): lax.all_gather(w_key[0], 'seq', axis=0, tiled=True)]
    all_to_all x0 -> x1, starting transfers between devices: none -> 12.3 us  [body(): lax.all_to_all(jnp.stack([w_query[0]] * lax.axis_size('seq'), 0), 'seq',...]
    reshape x0 -> x1, local copies, waits for them, and re-layouts: none -> 12.3 us  [body(): jnp.concatenate(lax.all_to_all(jnp.stack([w_query[0]] * lax.axis_size('se...]
    another operation x0 -> x1, local copies, waits for them, and re-layouts: none -> 7.06 us  [body(): jnp.stack([w_query[0]] * lax.axis_size('seq'), 0)]
  transfers between devices with their start and end apart: 7 -> 7, of which waited for: 5 -> 5; matrix products, arithmetic and copies ran while one was open for 27% -> 20% of each run, Pallas kernels for 0% -> 0%
where the time goes in v1:
time: 480 us; the launch traced here: 478 us
  waiting for transfers between devices  322 us (67%)
  local copies, waits for them, and re-layouts  58.4 us (12%)
  matrix products  51.4 us (11%)
  starting transfers between devices  16.7 us (3%)
  between operations  14 us (3%)
  other arithmetic  10.4 us (2%)
  loops' own time  5.3 us (1%)
    all_gather x1, waiting for transfers between devices, body(): lax.all_gather(w_value[0], 'seq', axis=0, tiled=True)  120 us
    all_gather x1, waiting for transfers between devices, body(): lax.all_gather(w_key[0], 'seq', axis=0, tiled=True)  98.9 us
    all_to_all x1, waiting for transfers between devices, body(): lax.all_to_all(jnp.stack([w_query[0]] * lax.axis_size('seq'), 0), 'seq',...  52.2 us
    psum x1, waiting for transfers between devices, body(): lax.psum(verdict.astype(jnp.bfloat16), 'member').astype(jnp.float32)  47.2 us
    dot_general x1, local copies, waits for them, and re-layouts, body(): jnp.dot(normed, jnp.concatenate(lax.all_to_all(jnp.stack([w_query[0]] * l...  16.4 us
    all_to_all x1, starting transfers between devices, body(): lax.all_to_all(jnp.stack([w_query[0]] * lax.axis_size('seq'), 0), 'seq',...  12.3 us
    reshape x1, local copies, waits for them, and re-layouts, body(): jnp.concatenate(lax.all_to_all(jnp.stack([w_query[0]] * lax.axis_size('se...  12.3 us
    dot_general x4, matrix products, one_head(): jnp.einsum('qgd,kd->gqk', query_head, key_head, preferred_element_type=jn...  12.1 us
  transfers between devices with their start and end apart: 7, of which 5 were waited for; matrix products, arithmetic and copies ran while one was open for 20% of the time, Pallas kernels for 0%

profile of v1, /device:TPU:2, one launch (start us, length us, event | category | flops | bytes accessed | tf_op | source)
XLA Modules:
  0.0 478.0 jit_solution(7381313044075834169)
XLA Ops:
  7.2 7.1 %stack.3 = bf16[64,45,2048]{2,1,0:T(8,128)(2,1)} broadcast(bf16[45,2048]{1,0:T(8,128)(2,1)} %bitcast.107), dimensions={1,2} | broadcast | bytes 11980800 | tf_op jit(solution)/shard_map/stack | solution.py:91
  14.3 12.3 %all-to-all-start = ((bf16[64,45,2048]{2,1,0:T(8,128)(2,1)}), bf16[64,45,2048]{2,1,0:T(8,128)(2,1)}, u32[]{:S(2)}, u32[]{:S(2)}) async-start(bf16[64,45,2048]{2,1,0:T(8,128)(2,1)} %stack.3), calls=%async_computation | async-start | bytes 25165824 | tf_op jit(solution)/shard_map/all_to_all | solution.py:91
  26.6 0.0 all-gather.7.cloned.1.call-start
  26.7 0.7 copy.27
  27.4 0.0 all-gather.9.cloned.1.call-start
  27.4 0.7 copy.28
  28.1 0.0 all-gather.11.cloned.1.call-start
  28.2 0.7 all-gather.11.cloned.1.call-update
  28.8 0.0 all-reduce.2.cloned.1.call-start
  29.1 0.8 dynamic_slice.19
  29.8 0.8 broadcast_select_fusion
  30.7 0.6 fusion.27
  31.2 0.3 multiply_cosine_fusion
  31.5 120.2 %all-gather.7.cloned.1.call-done = bf16[1,2880,256]{2,0,1:T(2,128)(2,1)} async-done(((bf16[1,45,256]{2,0,1:T(2,128)(2,1)}), bf16[1,2880,256]{2,0,1:T(2,128)(2,1)}) %all-gather.7.cloned.1.call-update) | async-done | bytes 1474576 | tf_op jit(solution)/shard_map/all_gather | solution.py:102
  151.7 3.2 fusion.45
  154.9 0.7 copy-done.3
  155.6 2.1 collective-permute-start
  157.7 98.9 %all-gather.9.cloned.1.call-done = bf16[1,2880,256]{2,0,1:T(2,128)(2,1)} async-done(((bf16[1,45,256]{2,0,1:T(2,128)(2,1)}), bf16[1,2880,256]{2,0,1:T(2,128)(2,1)}) %all-gather.9.cloned.1.call-update) | async-done | bytes 1474576 | tf_op jit(solution)/shard_map/all_gather | solution.py:97
  256.6 7.3 %copy.35 = bf16[1,2880,256]{1,2,0:T(8,128)(2,1)} copy(bf16[1,2880,256]{2,0,1:T(2,128)(2,1)} %all-gather.9.cloned.1.call-done) | data formatting | bytes 2949120 | tf_op jit(solution)/shard_map/dot_general | solution.py:95
  263.9 2.5 fusion.56
  266.4 0.1 multiply_subtract_fusion.1
  266.5 0.6 slice.31
  267.1 2.1 collective-permute-start.1
  269.3 0.9 pad_maximum_fusion
  270.1 0.9 copy.31
  271.0 2.5 collective-permute-done.1
  273.5 1.6 pad_maximum_fusion.1
  275.1 52.2 %all-to-all-done = bf16[64,45,2048]{2,1,0:T(8,128)(2,1)} async-done(((bf16[64,45,2048]{2,1,0:T(8,128)(2,1)}), bf16[64,45,2048]{2,1,0:T(8,128)(2,1)}, u32[]{:S(2)}, u32[]{:S(2)}) %all-to-all-start) | async-done | bytes 11796512 | tf_op jit(solution)/shard_map/all_to_all | solution.py:91
  327.3 12.3 %reshape.157 = bf16[2880,2048]{1,0:T(8,128)(2,1)} reshape(bf16[64,45,2048]{2,1,0:T(8,128)(2,1)} %all-to-all-done) | data formatting | bytes 23592960 | tf_op jit(solution)/shard_map/reshape | solution.py:90
  339.6 16.4 %copy.30 = bf16[2048,2880]{1,0:T(8,128)(2,1)} copy(bf16[2048,2880]{0,1:T(8,128)(2,1)} %bitcast.99) | data formatting | bytes 23592960 | tf_op jit(solution)/shard_map/dot_general | solution.py:88
  356.0 9.7 %fusion.54 = f32[384,32,64]{0,2,1:T(8,128)S(1)} fusion(bf16[32,64,2880]{2,1,0:T(8,128)(2,1)} %bitcast.100, bf16[1,384,2880]{1,2,0:T(8,128)(2,1)S(1)} %copy-done.1, f32[2880]{0:T(1024)S(1)} %reduce, f32[384]{0:T(512)S(1)} %copy-done.11), kind=kOutput, calls=%fused_computation.58 | convolution fusion | flops 4534272000 | bytes 17167104 | tf_op jit(solution)/shard_map/dot_general | solution.py:88
  365.7 0.4 multiply_subtract_fusion
  366.2 1.5 fusion.33
  367.7 40.1 %while.18 = (s32[]{:T(128)}, bf16[4,384,512]{1,2,0:T(8,128)(2,1)}, s32[4]{0:T(128)S(1)}, bf16[512,256]{0,1:T(8,128)(2,1)}, bf16[512,256]{0,1:T(8,128)(2,1)}, /*i...) while((s32[]{:T(128)}, bf16[4,384,512]{1,2,0:T(8,128)(2,1)}, ...), condition=%wide.region_3.4_spmd.clone, body=%wide.region_1.3_spmd.clone.sunk | while | flops 418182144 | bytes 15693569 | solution.py:75
  367.7 0.6 dynamic_slice.44
  368.9 1.1 constant_dynamic-slice_fusion.2
  370.7 0.3 fusion.70
  371.0 3.0 fusion.71
  374.0 3.0 fusion.72
  377.0 0.8 constant_dynamic-update-slice_fusion.2
  377.7 0.6 dynamic_slice.44
  379.0 1.0 constant_dynamic-slice_fusion.2
  380.7 0.3 fusion.70
  381.0 3.0 fusion.71
  384.0 3.0 fusion.72
  387.0 0.8 constant_dynamic-update-slice_fusion.2
  387.8 0.6 dynamic_slice.44
  389.0 1.0 constant_dynamic-slice_fusion.2
  390.7 0.3 fusion.70
  391.0 3.0 fusion.71
  394.0 3.0 fusion.72
  397.0 0.8 constant_dynamic-update-slice_fusion.2
  397.8 0.6 dynamic_slice.44
  399.0 1.0 constant_dynamic-slice_fusion.2
  400.7 0.3 fusion.70
  401.0 3.0 fusion.71
  404.1 3.0 fusion.72
  407.0 0.8 constant_dynamic-update-slice_fusion.2
  407.8 10.0 %multiply_reduce_fusion = (f32[384]{0:T(512)S(1)}, f32[384,2880]{0,1:T(8,128)S(1)}) fusion(bf16[384,2048]{0,1:T(8,128)(2,1)} %bitcast.12, bf16[1,2048,2880]{2,1,0:T(8,128)(2,1)} %all-gather.11.cloned.1.call-done), kind=kOutput, calls=%fused_computation.41 | convolution fusion | flops 4532059648 | bytes 17794560 | tf_op jit(solution)/shard_map/dot_general | solution.py:135
  417.8 1.5 fusion.24
  419.3 1.3 copy-done.2
  420.7 2.1 fusion.50
  422.8 47.2 %all-reduce.2.cloned.1.call-done = bf16[384,128]{1,0:T(8,128)(2,1)} async-done(((bf16[384,128]{1,0:T(8,128)(2,1)}), bf16[384,128]{1,0:T(8,128)(2,1)}) %all-reduce.2.cloned.1.call-update) | async-done | bytes 98320 | tf_op jit(solution)/shard_map/psum | solution.py:145
  469.9 1.6 convert_multiply_fusion.3
  (41 shorter events, 0.3 us)
Async XLA Ops:
  7.2 413.5 %copy-start = (bf16[1,2880,128]{2,1,0:T(8,128)(2,1)S(1)}, bf16[1,2880,128]{2,1,0:T(8,128)(2,1)}, u32[]{:S(2)}) copy-start(bf16[1,2880,128]{2,1,0:T(8,128)(2,1)} %param.21) | copy-start | bytes 2211844
  14.2 12.4 %copy-start.5 = (bf16[1,45,256]{2,1,0:T(8,128)(2,1)S(1)}, bf16[1,45,256]{2,1,0:T(8,128)(2,1)}, u32[]{:S(2)}) copy-start(bf16[1,45,256]{2,1,0:T(8,128)(2,1)} %param.17) | copy-start | bytes 69124
  14.2 13.2 %copy-start.6 = (bf16[1,45,256]{2,1,0:T(8,128)(2,1)S(1)}, bf16[1,45,256]{2,1,0:T(8,128)(2,1)}, u32[]{:S(2)}) copy-start(bf16[1,45,256]{2,1,0:T(8,128)(2,1)} %param.16) | copy-start | bytes 69124
  14.2 14.7 %copy-start.7 = (f32[1,2880]{1,0:T(1,128)S(1)}, f32[1,2880]{1,0:T(1,128)}, u32[]{:S(2)}) copy-start(f32[1,2880]{1,0:T(1,128)} %param.14) | copy-start | bytes 34564
  14.2 14.7 %copy-start.8 = (f32[1,2880]{1,0:T(1,128)S(1)}, f32[1,2880]{1,0:T(1,128)}, u32[]{:S(2)}) copy-start(f32[1,2880]{1,0:T(1,128)} %param.19) | copy-start | bytes 34564
  14.3 14.8 %copy-start.9 = (f32[1,2880]{1,0:T(1,128)S(1)}, f32[1,2880]{1,0:T(1,128)}, u32[]{:S(2)}) copy-start(f32[1,2880]{1,0:T(1,128)} %param.20) | copy-start | bytes 34564
  14.3 16.4 %copy-start.1 = (bf16[1,384,2880]{1,2,0:T(8,128)(2,1)S(1)}, bf16[1,384,2880]{1,2,0:T(8,128)(2,1)}, u32[]{:S(2)}) copy-start(bf16[1,384,2880]{1,2,0:T(8,128)(2,1)} %param.12) | copy-start | bytes 6635524
  14.3 313.0 %all-to-all-start = ((bf16[64,45,2048]{2,1,0:T(8,128)(2,1)}), bf16[64,45,2048]{2,1,0:T(8,128)(2,1)}, u32[]{:S(2)}, u32[]{:S(2)}) async-start(bf16[64,45,2048]{2,1,0:T(8,128)(2,1)} %stack.3), calls=%async_computation | async-start | bytes 25165824 | tf_op jit(solution)/shard_map/all_to_all | solution.py:91
  26.6 125.1 %all-gather.7.cloned.1.call-start = ((), (), s32[]{:S(2)}) async-start(), calls=%async_computation.2 | async-start | bytes 2995200 | tf_op jit(solution)/shard_map/all_gather | solution.py:102
  27.4 229.3 %all-gather.9.cloned.1.call-start = ((), (), s32[]{:S(2)}) async-start(), calls=%async_computation.3 | async-start | bytes 2995200 | tf_op jit(solution)/shard_map/all_gather | solution.py:97
  28.1 379.7 %all-gather.11.cloned.1.call-start = ((), (), s32[]{:S(2)}) async-start(), calls=%async_computation.4 | async-start | bytes 12247040 | tf_op jit(solution)/shard_map/all_gather | solution.py:137
  28.8 441.1 %all-reduce.2.cloned.1.call-start = ((), (), s32[]{:S(2)}) async-start(), calls=%async_computation.1 | async-start | bytes 196608 | tf_op jit(solution)/shard_map/psum | solution.py:145
  31.2 232.7 %copy-start.10 = (f32[384]{0:T(512)}, f32[384]{0:T(512)S(1)}, u32[]{:S(2)}) copy-start(f32[384]{0:T(512)S(1)} %add_rsqrt_fusion.2) | copy-start | bytes 4612
  154.9 0.7 copy-start.3
  155.6 113.7 %collective-permute-start = (bf16[128,256]{1,0:T(8,128)(2,1)S(1)}, bf16[128,256]{1,0:T(8,128)(2,1)}, u32[]{:S(2)}, u32[]{:S(2)}) collective-permute-start(bf16[128,256]{1,0:T(8,128)(2,1)S(1)} %slice.28), channel_id=1, source_target_pairs={{0,1},{1,2},{2,3},{3,4},{4,5},{5,6},{6,7},{7,8},{8,9},{9,10},{10,1... | collective-permute-start | bytes 196616 | tf_op jit(solution)/shard_map/ppermute | solution.py:19
  263.9 5.4 %copy-start.4 = (bf16[384,256]{1,0:T(8,128)(2,1)S(1)}, bf16[384,256]{1,0:T(8,128)(2,1)}, u32[]{:S(2)}) copy-start(bf16[384,256]{1,0:T(8,128)(2,1)} %copy-done.3) | copy-start | bytes 589828
  267.1 6.4 %collective-permute-start.1 = (bf16[128,256]{0,1:T(8,128)(2,1)}, bf16[128,256]{0,1:T(8,128)(2,1)}, u32[]{:S(2)}, u32[]{:S(2)}) collective-permute-start(bf16[128,256]{0,1:T(8,128)(2,1)} %bitcast.5), channel_id=1, source_target_pairs={{0,1},{1,2},{2,3},{3,4},{4,5},{5,6},{6,7},{7,8},{8,9},{9,10},{10,1... | collective-permute-start | bytes 196616 | tf_op jit(solution)/shard_map/ppermute | solution.py:19
  339.6 16.4 %copy-start.11 = (f32[384]{0:T(512)S(1)}, f32[384]{0:T(512)}, u32[]{:S(2)}) copy-start(f32[384]{0:T(512)} %copy-done.10) | copy-start | bytes 4612
  419.3 1.4 copy-start.2
Sparse Core Ops, SparseCore 0:
  30.7 120.9 all-gather.6
  154.4 102.1 all-gather.8
  259.3 118.9 all-gather.10
  422.9 46.9 all-reduce.1
